TPU v7x, 256 devices: a whole 4x4x8 slice. The times are simulated.
256 devices in a mesh: row: 16 (over z, core), col: 16 (over x, y).
Axes of the slice: x: 4, y: 4, z: 8, core: 2. Of those that a mesh axis runs over, the one named last changes fastest.
Arguments:
- tile_values: float32 [12288, 32, 1024], P(('row', 'col')), may hold values from -6 to 6
- tile_count: int32 [256], P(('row', 'col')), may hold values from 1 to 48, as said below
- mode1_column: int32 [12288, 1], P(('row', 'col')), may hold values from 0 to 15; in each aligned block of 48 rows (0 to 47, 48 to 95, ...) at most 4 rows name the same one
- mode1_offset: int32 [12288], P(('row', 'col')), may hold values from 0 to 15
- mode2_row: int32 [12288, 1], P(('row', 'col')), may hold values from 0 to 15; in each aligned block of 48 rows (0 to 47, 48 to 95, ...) at most 4 rows name the same one
- mode2_offset: int32 [12288], P(('row', 'col')), may hold values from 0 to 7
- mode3_offset: int32 [12288], P(('row', 'col')), may hold values from 0 to 15
- mode2_factor: float32 [65536, 256], P(('row', 'col'))
- mode3_factor: float32 [8192, 256], P('col')
Outputs:
- updated: float32 [131072, 256], P(('row', 'col'))
Inputs may be any that keep to these rules, and one draw needn't show every extreme that they name: Device d's live tiles fill its first tile_count[d] slots; other slots are ignored. Some device holds 48 live tiles. `mode1_column`: at most 4 slots of one device name the same value, and some device reaches it. `mode2_row`: at most 4 slots of one device name the same value, and some device reaches it.
All inputs are finite; a program needn't handle non-finite values.
Results may differ from a plain program's by a relative error of at most 0.0003.
Values sent between devices are 32-bit elements; how exact they have to be, the bound alone decides.
No kernel may reach another device: no remote copies, remote signals or barrier semaphores. Data moves between devices by JAX's collectives and lax.ppermute only.
A program may use at most 128 MiB of HBM per device.

v0:
```python
import jax
import jax.numpy as jnp
from jax import lax
from jax.sharding import PartitionSpec as P

IB_DEV = 16
HIGHEST_PRECISION = lax.Precision.HIGHEST


def product_of(left_matrix, right_matrix):
    return lax.dot_general(
        left_matrix,
        right_matrix,
        (((0,), (0,)), ((), ())),
        precision=HIGHEST_PRECISION,
        preferred_element_type=jnp.float32,
    )


def local(
    tile_values,
    tile_count,
    mode1_column,
    mode1_offset,
    mode2_row,
    mode2_offset,
    mode3_offset,
    mode2_factor,
    mode3_factor,
):
    slot_count = tile_values.shape[0]
    tile_edge = tile_values.shape[1]
    rank_width = mode2_factor.shape[1]
    rows_held = mode2_factor.shape[0]
    col_index = lax.axis_index("col")
    live_count = tile_count[0]
    slot_index = jnp.arange(slot_count, dtype=jnp.int32)
    is_live = slot_index < live_count
    tile_lines = jnp.arange(tile_edge, dtype=jnp.int32)
    owner_row = jnp.where(is_live, mode2_row[:, 0], -1)
    owner_col = jnp.where(is_live, mode1_column[:, 0], -1)
    own_second = product_of(mode2_factor, mode2_factor)
    own_third = product_of(mode3_factor, mode3_factor)
    sum_second = lax.psum(own_second, ("row", "col"))
    sum_third = lax.psum(own_third, "col")
    normal_matrix = sum_second * sum_third
    wanted = (owner_row * rows_held + mode2_offset * tile_edge)[:, None] + tile_lines[None, :]
    shard_piece = lax.all_gather(mode2_factor, "row", axis=0, tiled=True)
    piece_length = shard_piece.shape[0]
    inside = (wanted >= 0) & (wanted < piece_length)
    taken = jnp.take(shard_piece, jnp.clip(wanted, 0, piece_length - 1).reshape(-1), axis=0)
    taken = taken.reshape(slot_count, tile_edge, rank_width)
    picked = jnp.where(inside[:, :, None], taken, 0.0)
    third_index = (mode3_offset * tile_edge)[:, None] + tile_lines[None, :]
    mode3_rows = jnp.take(mode3_factor, third_index.reshape(-1), axis=0).reshape(
        slot_count, tile_edge, rank_width
    )
    group_size = min(8, slot_count)
    group_total = (live_count + group_size - 1) // group_size

    def contract(group_at, partials):
        start_slot = jnp.minimum(group_at * group_size, slot_count - group_size).astype(jnp.int32)
        second_part = lax.dynamic_slice_in_dim(picked, start_slot, group_size, 0)
        third_part = lax.dynamic_slice_in_dim(mode3_rows, start_slot, group_size, 0)
        values_part = lax.dynamic_slice_in_dim(tile_values, start_slot, group_size, 0)
        khatri = (second_part[:, :, None, :] * third_part[:, None, :, :]).reshape(
            group_size, tile_edge * tile_edge, rank_width
        )
        product_rows = jnp.einsum("gie,ger->gir", values_part, khatri, precision=HIGHEST_PRECISION)
        return lax.dynamic_update_slice_in_dim(partials, product_rows, start_slot, 0)

    partials = lax.fori_loop(
        0, group_total, contract, jnp.zeros((slot_count, tile_edge, rank_width), jnp.float32)
    )
    sent_targets = jnp.where(is_live, owner_col * IB_DEV + mode1_offset, -1).astype(jnp.float32)
    own_blocks = (col_index * IB_DEV + jnp.arange(IB_DEV, dtype=jnp.int32)).astype(jnp.float32)
    gathered_rows = lax.all_gather(partials, "col", axis=0, tiled=True)
    gathered_targets = lax.all_gather(sent_targets, "col", axis=0, tiled=True)
    selector = (gathered_targets[:, None] == own_blocks[None, :]).astype(jnp.float32)
    mttkrp = jnp.einsum("pb,pir->bir", selector, gathered_rows, precision=HIGHEST_PRECISION)
    cholesky_factor = jnp.linalg.cholesky(normal_matrix)
    mttkrp_rows = mttkrp.reshape(IB_DEV * tile_edge, rank_width)
    return jax.scipy.linalg.cho_solve((cholesky_factor, True), mttkrp_rows.T).T


def solution(mesh):
    placed = (
        P(("row", "col"), None, None),
        P(("row", "col")),
        P(("row", "col"), None),
        P(("row", "col")),
        P(("row", "col"), None),
        P(("row", "col")),
        P(("row", "col")),
        P(("row", "col"), None),
        P("col", None),
    )
    return jax.shard_map(
        local, mesh=mesh, in_specs=placed, out_specs=P(("row", "col"), None), check_vma=False
    )
```

profile of v0, /device:TPU:1, one launch (start us, length us, event | category | flops | bytes accessed | tf_op | source)
XLA Modules:
  0.0 551.6 jit_solution(1135849408825072373)
XLA Ops:
  8.2 2.3 fusion.31
  10.6 1.7 fusion.32
  13.7 3.7 gather_fusion.1
  17.4 1.5 broadcast_select_fusion
  18.8 37.9 %all-gather.3.cloned.1.call-done = f32[4096,256]{1,0:T(8,128)} async-done(((f32[256,256]{1,0:T(8,128)}), f32[4096,256]{1,0:T(8,128)}) %all-gather.3.cloned.1.call-update) | async-done | bytes 4194320 | tf_op jit(solution)/shard_map/all_gather | solution.py:48
  56.7 5.9 %gather_fusion = f32[1536,256]{1,0:T(8,128)S(1)} fusion(f32[4096,256]{1,0:T(8,128)} %all-gather.3.cloned.1.call-done, s32[2048]{0:T(1024)S(1)} %pad_clamp_fusion.1), kind=kCustom, calls=%fused_computation | custom fusion | bytes 3151872 | tf_op jit(solution)/shard_map/jit(_take)/gather | solution.py:51
  62.6 1.5 select_select_fusion
  64.2 53.0 %while.11 = (s32[]{:T(128)}, f32[48,32,256]{2,0,1:T(8,128)S(1)}, s32[]{:T(128)}, f32[48,32,1024]{2,1,0:T(8,128)}, f32[48,32,256]{2,1,0:T(8,128)}, /*index=5*/f32...) while((s32[]{:T(128)}, f32[48,32,256]{2,0,1:T(8,128)S(1)}, ...), condition=%wide.region_7.8_spmd, body=%wide.region_6.7_spmd.sunk | while | flops 807403520 | bytes 20709556 | solution.py:72
  65.3 1.2 broadcast_multiply_fusion.3
  66.5 6.1 %fusion.52 = f32[8,32,256]{2,1,0:T(8,128)S(1)} fusion(f32[8,1024,256]{2,1,0:T(8,128)S(1)} %bitcast.78, f32[48,32,1024]{2,1,0:T(8,128)} %get-tuple-element.177, s32[]{:T(128)S(6)} %select_n.118), kind=kOutput, calls=%fused_computation.3.clone.1 | convolution fusion | flops 805306368 | bytes 9699332 | tf_op jit(solution)/shard_map/while/body/gie,ger->gir/dot_general | solution.py:69
  74.2 1.2 broadcast_multiply_fusion.3
  75.3 6.1 %fusion.52 = f32[8,32,256]{2,1,0:T(8,128)S(1)} fusion(f32[8,1024,256]{2,1,0:T(8,128)S(1)} %bitcast.78, f32[48,32,1024]{2,1,0:T(8,128)} %get-tuple-element.177, s32[]{:T(128)S(6)} %select_n.118), kind=kOutput, calls=%fused_computation.3.clone.1 | convolution fusion | flops 805306368 | bytes 9699332 | tf_op jit(solution)/shard_map/while/body/gie,ger->gir/dot_general | solution.py:69
  83.0 1.2 broadcast_multiply_fusion.3
  84.2 6.1 %fusion.52 = f32[8,32,256]{2,1,0:T(8,128)S(1)} fusion(f32[8,1024,256]{2,1,0:T(8,128)S(1)} %bitcast.78, f32[48,32,1024]{2,1,0:T(8,128)} %get-tuple-element.177, s32[]{:T(128)S(6)} %select_n.118), kind=kOutput, calls=%fused_computation.3.clone.1 | convolution fusion | flops 805306368 | bytes 9699332 | tf_op jit(solution)/shard_map/while/body/gie,ger->gir/dot_general | solution.py:69
  91.9 1.2 broadcast_multiply_fusion.3
  93.0 6.1 %fusion.52 = f32[8,32,256]{2,1,0:T(8,128)S(1)} fusion(f32[8,1024,256]{2,1,0:T(8,128)S(1)} %bitcast.78, f32[48,32,1024]{2,1,0:T(8,128)} %get-tuple-element.177, s32[]{:T(128)S(6)} %select_n.118), kind=kOutput, calls=%fused_computation.3.clone.1 | convolution fusion | flops 805306368 | bytes 9699332 | tf_op jit(solution)/shard_map/while/body/gie,ger->gir/dot_general | solution.py:69
  100.7 1.2 broadcast_multiply_fusion.3
  101.8 6.1 %fusion.52 = f32[8,32,256]{2,1,0:T(8,128)S(1)} fusion(f32[8,1024,256]{2,1,0:T(8,128)S(1)} %bitcast.78, f32[48,32,1024]{2,1,0:T(8,128)} %get-tuple-element.177, s32[]{:T(128)S(6)} %select_n.118), kind=kOutput, calls=%fused_computation.3.clone.1 | convolution fusion | flops 805306368 | bytes 9699332 | tf_op jit(solution)/shard_map/while/body/gie,ger->gir/dot_general | solution.py:69
  110.7 6.1 %fusion.52 = f32[8,32,256]{2,1,0:T(8,128)S(1)} fusion(f32[8,1024,256]{2,1,0:T(8,128)S(1)} %bitcast.78, f32[48,32,1024]{2,1,0:T(8,128)} %get-tuple-element.177, s32[]{:T(128)S(6)} %select_n.118), kind=kOutput, calls=%fused_computation.3.clone.1 | convolution fusion | flops 805306368 | bytes 9699332 | tf_op jit(solution)/shard_map/while/body/gie,ger->gir/dot_general | solution.py:69
  117.3 1.2 copy-done.1
  119.8 29.3 %all-reduce.1 = f32[768]{0:T(1024)S(1)} all-reduce(f32[768]{0:T(1024)S(1)} %convert_dynamic-update-slice_fusion), channel_id=1, replica_groups=mesh['row'=16,'col'=16] {'col'}, use_global_device_ids=true, to_apply=%add.1 | all-reduce | flops 768 | bytes 6144
  149.1 120.2 %all-reduce.5.cloned.1.call-done = f32[256,256]{0,1:T(8,128)} async-done(((f32[256,256]{0,1:T(8,128)}), f32[256,256]{0,1:T(8,128)}) %all-reduce.5.cloned.1.call-update) | async-done | bytes 262160 | tf_op jit(solution)/shard_map/psum | solution.py:44
  269.4 95.4 %all-reduce.7.cloned.1.call-done = f32[256,256]{0,1:T(8,128)} async-done(((f32[256,256]{0,1:T(8,128)}), f32[256,256]{0,1:T(8,128)}) %all-reduce.7.cloned.1.call-update) | async-done | bytes 262160 | tf_op jit(solution)/shard_map/psum | solution.py:45
  366.0 11.7 %cholesky.50 = f32[128,128]{1,0:T(8,128)S(1)} custom-call(f32[128,128]{1,0:T(8,128)S(1)} %cholesky.118), custom_call_target="Cholesky" | custom-call | tf_op jit(solution)/shard_map/jit(cholesky)/cholesky | solution.py:81
  377.8 9.8 %custom-call.18 = f32[1,128,128]{1,2,0:T(8,128)S(1)} custom-call(f32[1,128,128]{2,1,0:T(8,128)S(1)} %get-tuple-element.74), custom_call_target="InvertDiagBlocksLowerTriangular" | custom-call | tf_op jit(solution)/shard_map/jit(cholesky)/cholesky | solution.py:81
  388.1 11.7 %cholesky.105 = f32[128,128]{1,0:T(8,128)S(1)} custom-call(f32[128,128]{1,0:T(8,128)S(1)} %convolution_subtract_fusion.2), custom_call_target="Cholesky" | custom-call | tf_op jit(solution)/shard_map/jit(cholesky)/cholesky | solution.py:81
  402.0 4.3 while.12
  402.8 1.4 bitcast_dynamic-update-slice_fusion.2
  404.9 1.4 bitcast_dynamic-update-slice_fusion.2
  406.3 19.7 %custom-call.19 = f32[2,128,128]{1,2,0:T(8,128)S(1)} custom-call(f32[2,128,128]{2,1,0:T(8,128)S(1)} %get-tuple-element.46), custom_call_target="InvertDiagBlocksLowerTriangular" | custom-call | tf_op jit(solution)/shard_map/jit(_cho_solve)/triangular_solve | solution.py:83
  426.0 101.7 %all-gather.5.cloned.1.call-done = f32[768,32,256]{2,0,1:T(8,128)} async-done(((f32[48,32,256]{2,0,1:T(8,128)}), f32[768,32,256]{2,0,1:T(8,128)}) %all-gather.5.cloned.1.call-update) | async-done | bytes 25165840 | tf_op jit(solution)/shard_map/all_gather | solution.py:77
  527.7 12.3 %fusion.14 = f32[16,32,256]{2,0,1:T(8,128)S(1)} fusion(f32[768,32,256]{2,0,1:T(8,128)} %all-gather.5.cloned.1.call-done, f32[768]{0:T(1024)S(1)} %all-reduce.1, f32[16]{0:T(128)S(1)} %add_convert_fusion), kind=kOutput, calls=%fused_computation.39 | convolution fusion | flops 1207971840 | bytes 25693248 | tf_op jit(solution)/shard_map/pb,pir->bir/dot_general | solution.py:80
  (86 shorter events, 20.3 us)
Async XLA Ops:
  7.4 3.2 copy-start
  7.4 5.7 %copy-start.4 = (s32[48,1]{0,1:T(1,128)S(1)}, s32[48,1]{0,1:T(1,128)}, u32[]{:S(2)}) copy-start(s32[48,1]{0,1:T(1,128)} %param.15) | copy-start | bytes 580
  7.4 5.7 %copy-start.5 = (s32[48]{0:T(128)S(1)}, s32[48]{0:T(128)}, u32[]{:S(2)}) copy-start(s32[48]{0:T(128)} %param.16) | copy-start | bytes 580
  7.4 5.9 %copy-start.6 = (s32[48]{0:T(128)S(1)}, s32[48]{0:T(128)}, u32[]{:S(2)}) copy-start(s32[48]{0:T(128)} %param.17) | copy-start | bytes 580
  7.4 49.3 %all-gather.3.cloned.1.call-start = ((), (), s32[]{:S(2)}) async-start(), calls=%async_computation.2 | async-start | bytes 4456448 | tf_op jit(solution)/shard_map/all_gather | solution.py:48
  8.1 261.3 %all-reduce.5.cloned.1.call-start = ((), (), s32[]{:S(2)}) async-start(), calls=%async_computation | async-start | bytes 524288 | tf_op jit(solution)/shard_map/psum | solution.py:44
  10.5 354.3 %all-reduce.7.cloned.1.call-start = ((), (), s32[]{:S(2)}) async-start(), calls=%async_computation.1 | async-start | bytes 524288 | tf_op jit(solution)/shard_map/psum | solution.py:45
  12.3 515.3 %all-gather.5.cloned.1.call-start = ((), (), s32[]{:S(2)}) async-start(), calls=%async_computation.3 | async-start | bytes 26738688 | tf_op jit(solution)/shard_map/all_gather | solution.py:77
  117.2 1.2 copy-start.1
  117.2 1.3 copy-start.7
  117.3 2.4 copy-start.2
  117.3 2.4 copy-start.3
Sparse Core Ops, SparseCore 0:
  10.2 46.4 all-gather.2
Sparse Core Ops, SparseCore 1:
  14.0 255.3 all-reduce.4
  272.4 92.3 all-reduce.6
  367.4 160.2 all-gather.4
where the time goes:
time: 552 us
  waiting for transfers between devices  356 us (64%)
  other arithmetic  65.2 us (12%)
  matrix products  56.1 us (10%)
  blocking collectives  29.3 us (5%)
  local copies, waits for them, and re-layouts  26.3 us (5%)
  between operations  18 us (3%)
    psum x1, waiting for transfers between devices, local(): sum_second = lax.psum(own_second, ('row', 'col'))  120 us
    all_gather x1, waiting for transfers between devices, local(): gathered_rows = lax.all_gather(partials, 'col', axis=0, tiled=True)  102 us
    psum x1, waiting for transfers between devices, local(): sum_third = lax.psum(own_third, 'col')  95.4 us
    all_gather x1, waiting for transfers between devices, local(): shard_piece = lax.all_gather(mode2_factor, 'row', axis=0, tiled=True)  37.9 us
    dot_general x6, matrix products, contract(): jnp.einsum('gie,ger->gir', values_part, khatri, precision=HIGHEST_PRECISION)  36.6 us
    another operation x6, other arithmetic, local(): cholesky_factor = jnp.linalg.cholesky(normal_matrix)  34 us
    unnamed x1, blocking collectives  29.3 us
    another operation x3, other arithmetic, local(): return jax.scipy.linalg.cho_solve((cholesky_factor, True), mttkrp_rows.T).T  19.7 us
  transfers between devices with their start and end apart: 4, of which 4 were waited for; matrix products, arithmetic and copies ran while one was open for 24% of the time, Pallas kernels for 0%

commit v1 on v0

--- a/solution.py
+++ b/solution.py
@@ -74,7 +74,9 @@
     )
     sent_targets = jnp.where(is_live, owner_col * IB_DEV + mode1_offset, -1).astype(jnp.float32)
     own_blocks = (col_index * IB_DEV + jnp.arange(IB_DEV, dtype=jnp.int32)).astype(jnp.float32)
-    gathered_rows = lax.all_gather(partials, "col", axis=0, tiled=True)
+    everything = jnp.stack(lax.axis_size("col") * [partials], axis=0)
+    even = lax.all_to_all(everything, axis_name="col", split_axis=0, concat_axis=0)
+    gathered_rows = jnp.concatenate(even, 0)
     gathered_targets = lax.all_gather(sent_targets, "col", axis=0, tiled=True)
     selector = (gathered_targets[:, None] == own_blocks[None, :]).astype(jnp.float32)
     mttkrp = jnp.einsum("pb,pir->bir", selector, gathered_rows, precision=HIGHEST_PRECISION)

time: 552 us -> 906 us (1.64)
  blocking collectives: 29.3 us -> 469 us
  waiting for transfers between devices: 356 us -> 247 us
  local copies, waits for them, and re-layouts: 26.3 us -> 46.8 us
    unnamed x1, blocking collectives: 29.3 us -> 469 us
    all_gather x1 -> x0, waiting for transfers between devices: 102 us -> none  [local(): gathered_rows = lax.all_gather(partials, 'col', axis=0, tiled=True)]
    another operation x6 -> x7, local copies, waits for them, and re-layouts: 4.06 us -> 15.5 us  [the longest x1 11.6 us: local(): everything = jnp.stack(lax.axis_size('col') * [partials], axis=0)]
    psum x1, waiting for transfers between devices: 120 us -> 110 us  [local(): sum_second = lax.psum(own_second, ('row', 'col'))]
    all_to_all x0 -> x1, local copies, waits for them, and re-layouts: none -> 9.95 us  [local(): lax.all_to_all(everything, axis_name='col', split_axis=0, concat_axis=0)]
  transfers between devices with their start and end apart: 4 -> 4, of which waited for: 4 -> 3; matrix products, arithmetic and copies ran while one was open for 24% -> 8% of each run, Pallas kernels for 0% -> 0%
where the time goes in v1:
time: 906 us; the launch traced here: 905 us
  blocking collectives  469 us (52%)
  waiting for transfers between devices  247 us (27%)
  other arithmetic  66.5 us (7%)
  matrix products  51 us (6%)
  local copies, waits for them, and re-layouts  46.8 us (5%)
  between operations  17.8 us (2%)
    unnamed x1, blocking collectives  469 us
    psum x1, waiting for transfers between devices, local(): sum_second = lax.psum(own_second, ('row', 'col'))  110 us
    psum x1, waiting for transfers between devices, local(): sum_third = lax.psum(own_third, 'col')  95.4 us
    all_gather x1, waiting for transfers between devices, local(): shard_piece = lax.all_gather(mode2_factor, 'row', axis=0, tiled=True)  40.6 us
    dot_general x6, matrix products, contract(): jnp.einsum('gie,ger->gir', values_part, khatri, precision=HIGHEST_PRECISION)  36.6 us
    another operation x6, other arithmetic, local(): cholesky_factor = jnp.linalg.cholesky(normal_matrix)  34 us
    another operation x3, other arithmetic, local(): return jax.scipy.linalg.cho_solve((cholesky_factor, True), mttkrp_rows.T).T  19.7 us
  transfers between devices with their start and end apart: 4, of which 3 were waited for; matrix products, arithmetic and copies ran while one was open for 8% of the time, Pallas kernels for 0%

profile of v1, /device:TPU:1, one launch (start us, length us, event | category | flops | bytes accessed | tf_op | source)
XLA Modules:
  0.0 905.0 jit_solution(6734943769744892875)
XLA Ops:
  10.5 3.7 gather_fusion.1
  14.4 1.4 broadcast_select_fusion
  15.8 40.6 %all-gather.2.cloned.1.call-done = f32[4096,256]{1,0:T(8,128)} async-done(((f32[256,256]{1,0:T(8,128)}), f32[4096,256]{1,0:T(8,128)}) %all-gather.2.cloned.1.call-update) | async-done | bytes 4194320 | tf_op jit(solution)/shard_map/all_gather | solution.py:48
  56.4 5.8 gather_fusion
  62.2 1.5 select_select_fusion
  63.9 53.0 %while.11 = (s32[]{:T(128)}, f32[48,32,256]{2,0,1:T(8,128)S(1)}, s32[]{:T(128)}, f32[48,32,1024]{2,1,0:T(8,128)}, f32[48,32,256]{2,1,0:T(8,128)}, /*index=5*/f32...) while((s32[]{:T(128)}, f32[48,32,256]{2,0,1:T(8,128)S(1)}, ...), condition=%wide.region_7.8_spmd, body=%wide.region_6.7_spmd.sunk | while | flops 807403520 | bytes 20709556 | solution.py:72
  65.0 1.2 broadcast_multiply_fusion.3
  66.2 6.1 fusion.52
  75.0 6.1 fusion.52
  82.7 1.2 broadcast_multiply_fusion.3
  83.8 6.1 fusion.52
  91.5 1.2 broadcast_multiply_fusion.3
  92.7 6.1 fusion.52
  100.3 1.2 broadcast_multiply_fusion.3
  101.5 6.1 fusion.52
  110.3 6.1 fusion.52
  116.9 11.6 %stack.2 = f32[16,48,32,256]{3,1,2,0:T(8,128)} broadcast(f32[48,32,256]{2,0,1:T(8,128)S(1)} %get-tuple-element.38), dimensions={1,2,3} | broadcast | bytes 26738688 | tf_op jit(solution)/shard_map/stack | solution.py:77
  128.5 6.7 all-to-all-start
  135.3 1.3 fusion.31
  136.7 1.7 fusion.32
  139.9 468.7 %all-reduce.1 = f32[768]{0:T(1024)S(1)} all-reduce(f32[768]{0:T(1024)S(1)} %convert_dynamic-update-slice_fusion), channel_id=1, replica_groups=mesh['row'=16,'col'=16] {'col'}, use_global_device_ids=true, to_apply=%add.1 | all-reduce | flops 768 | bytes 6144
  608.7 110.2 %all-reduce.5.cloned.1.call-done = f32[256,256]{0,1:T(8,128)} async-done(((f32[256,256]{0,1:T(8,128)}), f32[256,256]{0,1:T(8,128)}) %all-reduce.5.cloned.1.call-update) | async-done | bytes 262160 | tf_op jit(solution)/shard_map/psum | solution.py:44
  718.8 95.4 %all-reduce.7.cloned.1.call-done = f32[256,256]{0,1:T(8,128)} async-done(((f32[256,256]{0,1:T(8,128)}), f32[256,256]{0,1:T(8,128)}) %all-reduce.7.cloned.1.call-update) | async-done | bytes 262160 | tf_op jit(solution)/shard_map/psum | solution.py:45
  815.4 11.7 %cholesky.50 = f32[128,128]{1,0:T(8,128)S(1)} custom-call(f32[128,128]{1,0:T(8,128)S(1)} %cholesky.118), custom_call_target="Cholesky" | custom-call | tf_op jit(solution)/shard_map/jit(cholesky)/cholesky | solution.py:83
  827.2 9.8 %custom-call.18 = f32[1,128,128]{1,2,0:T(8,128)S(1)} custom-call(f32[1,128,128]{2,1,0:T(8,128)S(1)} %get-tuple-element.74), custom_call_target="InvertDiagBlocksLowerTriangular" | custom-call | tf_op jit(solution)/shard_map/jit(cholesky)/cholesky | solution.py:83
  837.5 11.7 %cholesky.105 = f32[128,128]{1,0:T(8,128)S(1)} custom-call(f32[128,128]{1,0:T(8,128)S(1)} %convolution_subtract_fusion.2), custom_call_target="Cholesky" | custom-call | tf_op jit(solution)/shard_map/jit(cholesky)/cholesky | solution.py:83
  851.3 4.1 while.12
  852.1 1.3 bitcast_dynamic-update-slice_fusion.2
  854.0 1.3 bitcast_dynamic-update-slice_fusion.2
  855.4 19.7 %custom-call.19 = f32[2,128,128]{1,2,0:T(8,128)S(1)} custom-call(f32[2,128,128]{2,1,0:T(8,128)S(1)} %get-tuple-element.46), custom_call_target="InvertDiagBlocksLowerTriangular" | custom-call | tf_op jit(solution)/shard_map/jit(_cho_solve)/triangular_solve | solution.py:85
  875.1 9.9 %copy.25 = f32[16,48,32,256]{3,1,0,2:T(8,128)S(1)} copy(f32[16,48,32,256]{3,1,2,0:T(8,128)} %all-to-all-done) | data formatting | bytes 50331648 | tf_op jit(solution)/shard_map/all_to_all | solution.py:78
  885.0 8.5 fusion.14
  (82 shorter events, 22.7 us)
Async XLA Ops:
  7.4 3.1 copy-start
  7.4 49.0 %all-gather.2.cloned.1.call-start = ((), (), s32[]{:S(2)}) async-start(), calls=%async_computation.3 | async-start | bytes 4456448 | tf_op jit(solution)/shard_map/all_gather | solution.py:48
  128.5 6.8 copy-start.1
  128.5 746.6 %all-to-all-start = ((f32[16,48,32,256]{3,1,2,0:T(8,128)}), f32[16,48,32,256]{3,1,2,0:T(8,128)}, u32[]{:S(2)}, u32[]{:S(2)}) async-start(f32[16,48,32,256]{3,1,2,0:T(8,128)} %stack.2), calls=%async_computation | async-start | bytes 50331648 | tf_op jit(solution)/shard_map/all_to_all | solution.py:78
  135.2 3.2 copy-start.4
  135.2 4.6 copy-start.2
  135.3 4.6 copy-start.3
  135.3 583.6 %all-reduce.5.cloned.1.call-start = ((), (), s32[]{:S(2)}) async-start(), calls=%async_computation.1 | async-start | bytes 524288 | tf_op jit(solution)/shard_map/psum | solution.py:44
  136.7 677.5 %all-reduce.7.cloned.1.call-start = ((), (), s32[]{:S(2)}) async-start(), calls=%async_computation.2 | async-start | bytes 524288 | tf_op jit(solution)/shard_map/psum | solution.py:45
Sparse Core Ops, SparseCore 0:
  10.0 46.3 all-gather.1
Sparse Core Ops, SparseCore 1:
  141.2 577.6 all-reduce.4
  721.9 92.3 all-reduce.6
